TPU v7x, 128 devices: a whole 4x4x4 slice. The times are simulated.
128 devices in a mesh: rows: 4 (over x), cols: 32 (over y, z, core).
Axes of the slice: x: 4, y: 4, z: 4, core: 2. Of those that a mesh axis runs over, the one named last changes fastest.
Arguments:
- weight: bfloat16 [8192, 16384], P('rows', 'cols'), may hold values from -0.046875 to 0.046875
- hess_inv: float32 [16384, 16384], P('rows', 'cols'), as said below
- selected: int32 [3, 64], replicated, may hold values from 0 to 16383, as said below
- block_mask: int32 [8192, 128], P('rows'), may hold values 0 or 1
- row_limits: int32 [8192], P('rows'), may hold values from 16 to 128
- calibration: bfloat16 [1024, 16384], P(None, 'cols'), may hold values from -6 to 6
Outputs:
- pruned: bfloat16 [8192, 16384], P('rows', 'cols')
- layer_error: float32 [8192, 1024], P('rows', 'cols')
Inputs may be any that keep to these rules, and one draw needn't show every extreme that they name: `selected`: all 192 entries differ; 0 and 16383 are among them. `hess_inv`: symmetric positive definite.
All inputs are finite; a program needn't handle non-finite values. No bound on the sum of `block_mask` on one device may be relied on, other than what follows from the above.
Results may differ from a plain program's by a relative error of at most 0.005.
Values may be sent and summed in bfloat16 or wider, within the bound.
A program may use at most 128 MiB of HBM per device.

v0:
```python
import jax
import jax.numpy as jnp
from jax import lax
from jax.sharding import PartitionSpec as P

STEPS = 3
BLK = 128


def local(weight, hess_inv, selected, block_mask, row_limits, calibration):
    rows_local, cols_local = hess_inv.shape
    out_local = weight.shape[0]
    row_offset = lax.axis_index("rows") * rows_local
    col_offset = lax.axis_index("cols") * cols_local
    refit = weight.astype(jnp.float32)
    inverse = hess_inv
    for iteration in range(STEPS):
        chosen = selected[iteration]
        row_place = chosen - row_offset
        row_inside = (row_place >= 0) & (row_place < rows_local)
        row_pick = jnp.where(
            row_inside[:, None],
            jnp.take(inverse, jnp.clip(row_place, 0, rows_local - 1), axis=0),
            0.0,
        )
        panel = lax.psum(row_pick, "rows")
        col_place = chosen - col_offset
        col_inside = (col_place >= 0) & (col_place < cols_local)
        col_index = jnp.clip(col_place, 0, cols_local - 1)
        inverse_pick = jnp.where(col_inside[None, :], jnp.take(inverse, col_index, axis=1), 0.0)
        refit_pick = jnp.where(col_inside[None, :], jnp.take(refit, col_index, axis=1), 0.0)
        square_pick = jnp.where(col_inside[None, :], jnp.take(panel, col_index, axis=1), 0.0)
        inverse_cols, refit_cols, square = lax.psum((inverse_pick, refit_pick, square_pick), "cols")
        factor = jnp.linalg.cholesky(square)
        coeffs = jax.scipy.linalg.cho_solve((factor, True), panel)
        refit = refit - jnp.dot(refit_cols, coeffs, precision=lax.Precision.HIGHEST)
        inverse = inverse - jnp.dot(inverse_cols, coeffs, precision=lax.Precision.HIGHEST)
    blocks_local = cols_local // BLK
    running_count = jnp.cumsum(block_mask, axis=1)
    retained = block_mask * (running_count <= row_limits[:, None]).astype(jnp.int32)
    own_blocks = lax.dynamic_slice_in_dim(
        retained, lax.axis_index("cols") * blocks_local, blocks_local, 1
    )
    masked = (
        refit.reshape(out_local, blocks_local, BLK) * own_blocks.astype(jnp.float32)[:, :, None]
    ).reshape(out_local, cols_local)
    pruned = masked.astype(jnp.bfloat16)
    difference = (weight.astype(jnp.float32) - masked).astype(jnp.bfloat16)
    widened = lax.all_to_all(difference, "cols", split_axis=0, concat_axis=1, tiled=True)
    row_result = lax.dot_general(
        widened,
        lax.all_gather(calibration, "cols", axis=1, tiled=True),
        (((1,), (1,)), ((), ())),
        preferred_element_type=jnp.float32,
    )
    layer_error = lax.all_to_all(
        row_result.astype(jnp.bfloat16), "cols", split_axis=1, concat_axis=0, tiled=True
    ).astype(row_result.dtype)
    return (pruned, layer_error)


def solution(mesh):
    placed = (
        P("rows", "cols"),
        P("rows", "cols"),
        P(),
        P("rows", None),
        P("rows"),
        P(None, "cols"),
    )
    return jax.shard_map(
        local,
        mesh=mesh,
        in_specs=placed,
        out_specs=(P("rows", "cols"), P("rows", "cols")),
        check_vma=False,
    )
```

profile of v0, /device:TPU:1, one launch (start us, length us, event | category | flops | bytes accessed | tf_op | source)
XLA Modules:
  0.0 925.9 jit_solution(10366670984295173127)
XLA Ops:
  22.2 9.0 copy.60
  37.1 19.3 %all-reduce.11.cloned.1.call-done = f32[64,512]{1,0:T(8,128)} async-done(((f32[64,512]{1,0:T(8,128)}), f32[64,512]{1,0:T(8,128)}) %all-reduce.11.cloned.1.call-update) | async-done | bytes 131088 | tf_op jit(solution)/shard_map/psum | solution.py:26
  58.1 123.4 %psum.79 = f32[64,64]{0,1:T(8,128)S(1)} all-reduce(f32[64,64]{0,1:T(8,128)S(1)} %bitcast_select_fusion.7), channel_id=1, replica_groups=mesh['rows'=4,'cols'=32] {'cols'}, use_global_device_ids=true, to_apply=%region_2.6 | all-reduce | flops 4096 | bytes 32768 | tf_op jit(solution)/shard_map/psum | solution.py:33
  181.6 5.8 cholesky.59
  188.7 4.9 custom-call.9
  195.2 6.2 convolution_subtract_fusion.3
  201.4 5.4 copy.59
  211.2 107.3 %all-reduce.19.cloned.1.call-done = (f32[2048,64]{0,1:T(8,128)}, f32[4096,64]{0,1:T(8,128)}) async-done(((f32[2048,64]{0,1:T(8,128)}, f32[4096,64]{0,1:T(8,128)}), (f32[2048,64]{0,1:T(8,128)}, f32[4096,64]{0,1:T(8,128)})) %all-reduce.19.cloned.1.call-update) | async-done | bytes 1572880 | tf_op jit(solution)/shard_map/psum | solution.py:33
  318.4 11.5 %convolution_subtract_fusion.1 = f32[4096,512]{1,0:T(8,128)} fusion(f32[4096,512]{1,0:T(8,128)} %param.18, f32[4096,64]{0,1:T(8,128)} %get-tuple-element.10, f32[64,512]{1,0:T(8,128)S(1)} %fusion.14), kind=kOutput, calls=%fused_computation.12 | convolution fusion | flops 1612709888 | bytes 17956864 | tf_op jit(solution)/shard_map/dot_general | solution.py:37
  330.0 8.9 copy.64
  349.7 33.0 %all-reduce.13.cloned.1.call-done = f32[64,512]{1,0:T(8,128)} async-done(((f32[64,512]{1,0:T(8,128)}), f32[64,512]{1,0:T(8,128)}) %all-reduce.13.cloned.1.call-update) | async-done | bytes 131088 | tf_op jit(solution)/shard_map/psum | solution.py:26
  384.4 123.3 %psum.83 = f32[64,64]{0,1:T(8,128)S(1)} all-reduce(f32[64,64]{0,1:T(8,128)S(1)} %bitcast_select_fusion.6), channel_id=1, replica_groups=mesh['rows'=4,'cols'=32] {'cols'}, use_global_device_ids=true, to_apply=%region_8.15 | all-reduce | flops 4096 | bytes 32768 | tf_op jit(solution)/shard_map/psum | solution.py:33
  507.8 5.8 cholesky.70
  521.4 6.8 convolution_subtract_fusion.2
  528.2 5.4 copy.63
  538.1 107.3 %all-reduce.17.cloned.1.call-done = (f32[2048,64]{0,1:T(8,128)}, f32[4096,64]{0,1:T(8,128)}) async-done(((f32[2048,64]{0,1:T(8,128)}, f32[4096,64]{0,1:T(8,128)}), (f32[2048,64]{0,1:T(8,128)}, f32[4096,64]{0,1:T(8,128)})) %all-reduce.17.cloned.1.call-update) | async-done | bytes 1572880 | tf_op jit(solution)/shard_map/psum | solution.py:33
  645.4 11.5 %convolution_subtract_fusion = f32[4096,512]{1,0:T(8,128)} fusion(f32[4096,512]{1,0:T(8,128)} %convolution_subtract_fusion.1, f32[4096,64]{0,1:T(8,128)} %get-tuple-element.6, f32[64,512]{1,0:T(8,128)S(1)} %fusion.9), kind=kOutput, calls=%fused_computation.11 | convolution fusion | flops 1612709888 | bytes 17956864 | tf_op jit(solution)/shard_map/dot_general | solution.py:37
  667.2 33.6 %all-reduce.15.cloned.1.call-done = f32[64,512]{1,0:T(8,128)} async-done(((f32[64,512]{1,0:T(8,128)}), f32[64,512]{1,0:T(8,128)}) %all-reduce.15.cloned.1.call-update) | async-done | bytes 131088 | tf_op jit(solution)/shard_map/psum | solution.py:26
  702.5 127.2 %psum.87 = f32[64,64]{0,1:T(8,128)S(1)} all-reduce(f32[64,64]{0,1:T(8,128)S(1)} %bitcast_select_fusion.5), channel_id=1, replica_groups=mesh['rows'=4,'cols'=32] {'cols'}, use_global_device_ids=true, to_apply=%region_12.19 | all-reduce | flops 4096 | bytes 32768 | tf_op jit(solution)/shard_map/psum | solution.py:33
  829.8 5.8 cholesky.81
  848.2 5.5 subtract_convert_fusion
  853.7 36.5 %all_to_all.32 = bf16[32,64,512]{2,1,0:T(8,128)(2,1)S(1)} all-to-all(bf16[32,64,512]{2,1,0:T(8,128)(2,1)S(1)} %bitcast.115), channel_id=1, replica_groups=mesh['rows'=4,'cols'=32] {'cols'}, dimensions={0} | all-to-all | bytes 4194304 | tf_op jit(solution)/shard_map/all_to_all | solution.py:49
  890.5 15.4 %convolution_convert_fusion = bf16[64,1024]{1,0:T(8,128)(2,1)S(1)} fusion(bf16[64,16384]{1,0:T(8,128)(2,1)S(1)} %bitcast.113, bf16[1024,16384]{1,0:T(8,128)(2,1)} %all-gather.2.cloned.1.call-done), kind=kOutput, calls=%fused_computation.17 | convolution fusion | flops 2147549184 | bytes 35782656 | tf_op jit(solution)/shard_map/dot_general | solution.py:50
  906.2 11.4 %all_to_all.33 = bf16[32,2,1024]{2,1,0:T(2,128)(2,1)S(1)} all-to-all(bf16[32,2,1024]{2,1,0:T(2,128)(2,1)S(1)} %reshape.238), channel_id=1, replica_groups=mesh['rows'=4,'cols'=32] {'cols'}, dimensions={0} | all-to-all | bytes 262144 | tf_op jit(solution)/shard_map/all_to_all | solution.py:56
  (93 shorter events, 81.1 us)
Async XLA Ops:
  7.2 49.2 %all-reduce.11.cloned.1.call-start = ((), (), s32[]{:S(2)}) async-start(), calls=%async_computation.3 | async-start | bytes 262144 | tf_op jit(solution)/shard_map/psum | solution.py:26
  13.7 181.4 %all-reduce.9.cloned.1.call-start = ((), (), s32[]{:S(2)}) async-start(), calls=%async_computation.2 | async-start | bytes 1048576 | tf_op jit(solution)/shard_map/psum | solution.py:33
  22.1 296.3 %all-reduce.19.cloned.1.call-start = ((), (), s32[]{:S(2)}) async-start(), calls=%async_computation.8 | async-start | bytes 3145728 | tf_op jit(solution)/shard_map/psum | solution.py:33
  35.9 159.3 %copy-start.1 = (bf16[2048,512]{1,0:T(8,128)(2,1)S(1)}, bf16[2048,512]{1,0:T(8,128)(2,1)}, u32[]{:S(2)}) copy-start(bf16[2048,512]{1,0:T(8,128)(2,1)} %param.17) | copy-start | bytes 6291460
  210.9 171.8 %all-reduce.13.cloned.1.call-start = ((), (), s32[]{:S(2)}) async-start(), calls=%async_computation.4 | async-start | bytes 262144 | tf_op jit(solution)/shard_map/psum | solution.py:26
  343.8 301.6 %all-reduce.17.cloned.1.call-start = ((), (), s32[]{:S(2)}) async-start(), calls=%async_computation.7 | async-start | bytes 3145728 | tf_op jit(solution)/shard_map/psum | solution.py:33
  537.8 163.0 %all-reduce.15.cloned.1.call-start = ((), (), s32[]{:S(2)}) async-start(), calls=%async_computation.5 | async-start | bytes 262144 | tf_op jit(solution)/shard_map/psum | solution.py:26
  656.9 9.0 copy-start.3
  661.8 228.7 %all-gather.2.cloned.1.call-start = ((), (), s32[]{:S(2)}) async-start(), calls=%async_computation.6 | async-start | bytes 34603008 | tf_op jit(solution)/shard_map/all_gather | solution.py:52
  841.9 6.4 copy-start
  841.9 6.4 copy-start.2
Sparse Core Ops, SparseCore 0:
  13.8 42.4 all-reduce.10
  59.6 107.1 all-reduce.8
  211.0 107.3 all-reduce.18
  343.9 38.7 all-reduce.12
  537.9 107.4 all-reduce.16
  661.9 38.8 all-reduce.14
  703.0 128.8 all-gather.1
where the time goes:
time: 927 us; the launch traced here: 926 us
  blocking collectives  422 us (46%)
  waiting for transfers between devices  301 us (32%)
  local copies, waits for them, and re-layouts  77.9 us (8%)
  matrix products  61.5 us (7%)
  other arithmetic  48.2 us (5%)
  between operations  14.5 us (2%)
    psum x3, blocking collectives, local(): lax.psum((inverse_pick, refit_pick, square_pick), 'cols')  374 us
    psum x3, waiting for transfers between devices, local(): lax.psum((inverse_pick, refit_pick, square_pick), 'cols')  215 us
    psum x3, waiting for transfers between devices, local(): panel = lax.psum(row_pick, 'rows')  85.9 us
    all_to_all x1, blocking collectives, local(): lax.all_to_all(difference, 'cols', split_axis=0, concat_axis=1, tiled=True)  36.5 us
    dot_general x2, matrix products, local(): jnp.dot(inverse_cols, coeffs, precision=lax.Precision.HIGHEST)  23.1 us
    another operation x9, other arithmetic, local(): factor = jnp.linalg.cholesky(square)  19.6 us
  transfers between devices with their start and end apart: 7, of which 5 were waited for; matrix products, arithmetic and copies ran while one was open for 8% of the time, Pallas kernels for 0%

commit v1 on v0

--- a/solution.py
+++ b/solution.py
@@ -23,7 +23,11 @@
             jnp.take(inverse, jnp.clip(row_place, 0, rows_local - 1), axis=0),
             0.0,
         )
-        panel = lax.psum(row_pick, "rows")
+
+        def fill_side(base_x):
+            return lax.all_gather(base_x, axis_name="rows").sum(axis=0)
+
+        panel = fill_side(row_pick)
         col_place = chosen - col_offset
         col_inside = (col_place >= 0) & (col_place < cols_local)
         col_index = jnp.clip(col_place, 0, cols_local - 1)

time: 927 us -> 866 us (0.934)
  waiting for transfers between devices: 301 us -> 209 us
  blocking collectives: 422 us -> 457 us
    psum x3 -> x0, waiting for transfers between devices: 85.9 us -> none  [local(): panel = lax.psum(row_pick, 'rows')]
    all_gather x0 -> x3, blocking collectives: none -> 35.6 us  [fill_side(): return lax.all_gather(base_x, axis_name='rows').sum(axis=0)]
  transfers between devices with their start and end apart: 7 -> 4, of which waited for: 5 -> 2; matrix products, arithmetic and copies ran while one was open for 8% -> 9% of each run, Pallas kernels for 0% -> 0%
where the time goes in v1:
time: 866 us; the launch traced here: 864 us
  blocking collectives  457 us (53%)
  waiting for transfers between devices  209 us (24%)
  local copies, waits for them, and re-layouts  76.4 us (9%)
  matrix products  58.6 us (7%)
  other arithmetic  48.3 us (6%)
  between operations  14.2 us (2%)
    psum x3, blocking collectives, local(): lax.psum((inverse_pick, refit_pick, square_pick), 'cols')  373 us
    psum x3, waiting for transfers between devices, local(): lax.psum((inverse_pick, refit_pick, square_pick), 'cols')  209 us
    all_to_all x1, blocking collectives, local(): lax.all_to_all(difference, 'cols', split_axis=0, concat_axis=1, tiled=True)  36.6 us
    all_gather x3, blocking collectives, fill_side(): return lax.all_gather(base_x, axis_name='rows').sum(axis=0)  35.6 us
    dot_general x2, matrix products, local(): jnp.dot(inverse_cols, coeffs, precision=lax.Precision.HIGHEST)  23 us
    another operation x9, other arithmetic, local(): factor = jnp.linalg.cholesky(square)  19.6 us
    dot_general x3, matrix products, local(): refit = refit - jnp.dot(refit_cols, coeffs, precision=lax.Precision.HIGHEST)  18.5 us
  transfers between devices with their start and end apart: 4, of which 2 were waited for; matrix products, arithmetic and copies ran while one was open for 9% of the time, Pallas kernels for 0%

profile of v1, /device:TPU:1, one launch (start us, length us, event | category | flops | bytes accessed | tf_op | source)
XLA Modules:
  0.0 864.2 jit_solution(348549514732969949)
XLA Ops:
  17.2 8.9 %copy.51 = f32[4096,512]{0,1:T(8,128)} copy(f32[4096,512]{1,0:T(8,128)} %param.18) | data formatting | bytes 16777216 | tf_op args[1]
  30.4 12.4 %all-gather = f32[256,512]{1,0:T(8,128)S(1)} all-gather(f32[64,512]{1,0:T(8,128)S(1)} %select_select_fusion.2), channel_id=2, replica_groups=mesh['rows'=4,'cols'=32] {'rows'}, dimensions={0}, use_global_device_ids=true | all-gather | bytes 655360 | tf_op jit(solution)/shard_map/all_gather | solution.py:28
  43.7 124.6 %psum.57 = f32[64,64]{0,1:T(8,128)S(1)} all-reduce(f32[64,64]{0,1:T(8,128)S(1)} %bitcast_select_fusion.7), channel_id=1, replica_groups=mesh['rows'=4,'cols'=32] {'cols'}, use_global_device_ids=true, to_apply=%region_2.6 | all-reduce | flops 4096 | bytes 32768 | tf_op jit(solution)/shard_map/psum | solution.py:37
  168.4 5.8 cholesky.59
  180.8 4.9 gather_fusion.4
  187.2 6.2 convolution_subtract_fusion.3
  193.4 5.4 copy.50
  203.1 106.4 %all-reduce.10.cloned.1.call-done = (f32[2048,64]{0,1:T(8,128)}, f32[4096,64]{0,1:T(8,128)}) async-done(((f32[2048,64]{0,1:T(8,128)}, f32[4096,64]{0,1:T(8,128)}), (f32[2048,64]{0,1:T(8,128)}, f32[4096,64]{0,1:T(8,128)})) %all-reduce.10.cloned.1.call-update) | async-done | bytes 1572880 | tf_op jit(solution)/shard_map/psum | solution.py:37
  309.6 11.5 %convolution_subtract_fusion.1 = f32[4096,512]{1,0:T(8,128)} fusion(f32[4096,512]{1,0:T(8,128)} %param.18, f32[4096,64]{0,1:T(8,128)} %get-tuple-element.10, f32[64,512]{1,0:T(8,128)S(1)} %fusion.14), kind=kOutput, calls=%fused_computation.12 | convolution fusion | flops 1612709888 | bytes 17956864 | tf_op jit(solution)/shard_map/dot_general | solution.py:41
  321.1 8.9 %copy.55 = f32[4096,512]{0,1:T(8,128)} copy(f32[4096,512]{1,0:T(8,128)} %convolution_subtract_fusion.1) | data formatting | bytes 16777216 | tf_op jit(solution)/shard_map/sub | solution.py:41
  334.2 11.4 %all-gather.1 = f32[256,512]{1,0:T(8,128)S(1)} all-gather(f32[64,512]{1,0:T(8,128)S(1)} %select_select_fusion.1), channel_id=3, replica_groups=mesh['rows'=4,'cols'=32] {'rows'}, dimensions={0}, use_global_device_ids=true | all-gather | bytes 655360 | tf_op jit(solution)/shard_map/all_gather | solution.py:28
  346.5 122.2 %psum.60 = f32[64,64]{0,1:T(8,128)S(1)} all-reduce(f32[64,64]{0,1:T(8,128)S(1)} %bitcast_select_fusion.6), channel_id=1, replica_groups=mesh['rows'=4,'cols'=32] {'cols'}, use_global_device_ids=true, to_apply=%region_8.15 | all-reduce | flops 4096 | bytes 32768 | tf_op jit(solution)/shard_map/psum | solution.py:37
  468.8 5.8 cholesky.70
  481.5 6.8 convolution_subtract_fusion.2
  488.3 5.4 copy.54
  509.0 102.4 %all-reduce.8.cloned.1.call-done = (f32[2048,64]{0,1:T(8,128)}, f32[4096,64]{0,1:T(8,128)}) async-done(((f32[2048,64]{0,1:T(8,128)}, f32[4096,64]{0,1:T(8,128)}), (f32[2048,64]{0,1:T(8,128)}, f32[4096,64]{0,1:T(8,128)})) %all-reduce.8.cloned.1.call-update) | async-done | bytes 1572880 | tf_op jit(solution)/shard_map/psum | solution.py:37
  611.4 11.5 %convolution_subtract_fusion = f32[4096,512]{1,0:T(8,128)} fusion(f32[4096,512]{1,0:T(8,128)} %convolution_subtract_fusion.1, f32[4096,64]{0,1:T(8,128)} %get-tuple-element.6, f32[64,512]{1,0:T(8,128)S(1)} %fusion.9), kind=kOutput, calls=%fused_computation.11 | convolution fusion | flops 1612709888 | bytes 17956864 | tf_op jit(solution)/shard_map/dot_general | solution.py:41
  627.6 11.8 %all-gather.2 = f32[256,512]{1,0:T(8,128)} all-gather(f32[64,512]{1,0:T(8,128)S(1)} %select_select_fusion), channel_id=4, replica_groups=mesh['rows'=4,'cols'=32] {'rows'}, dimensions={0}, use_global_device_ids=true | all-gather | bytes 655360 | tf_op jit(solution)/shard_map/all_gather | solution.py:28
  642.7 126.5 %psum.63 = f32[64,64]{0,1:T(8,128)S(1)} all-reduce(f32[64,64]{0,1:T(8,128)S(1)} %bitcast_select_fusion.5), channel_id=1, replica_groups=mesh['rows'=4,'cols'=32] {'cols'}, use_global_device_ids=true, to_apply=%region_12.19 | all-reduce | flops 4096 | bytes 32768 | tf_op jit(solution)/shard_map/psum | solution.py:37
  769.4 5.8 cholesky.81
  786.8 5.5 subtract_convert_fusion
  792.2 36.6 %all_to_all.32 = bf16[32,64,512]{2,1,0:T(8,128)(2,1)S(1)} all-to-all(bf16[32,64,512]{2,1,0:T(8,128)(2,1)S(1)} %bitcast.118), channel_id=1, replica_groups=mesh['rows'=4,'cols'=32] {'cols'}, dimensions={0} | all-to-all | bytes 4194304 | tf_op jit(solution)/shard_map/all_to_all | solution.py:53
  829.0 15.4 %convolution_convert_fusion = bf16[64,1024]{1,0:T(8,128)(2,1)S(1)} fusion(bf16[64,16384]{1,0:T(8,128)(2,1)S(1)} %bitcast.116, bf16[1024,16384]{1,0:T(8,128)(2,1)} %all-gather.5.cloned.1.call-done), kind=kOutput, calls=%fused_computation.17 | convolution fusion | flops 2147549184 | bytes 35782656 | tf_op jit(solution)/shard_map/dot_general | solution.py:54
  844.8 11.4 %all_to_all.33 = bf16[32,2,1024]{2,1,0:T(2,128)(2,1)S(1)} all-to-all(bf16[32,2,1024]{2,1,0:T(2,128)(2,1)S(1)} %reshape.241), channel_id=1, replica_groups=mesh['rows'=4,'cols'=32] {'cols'}, dimensions={0} | all-to-all | bytes 262144 | tf_op jit(solution)/shard_map/all_to_all | solution.py:60
  (90 shorter events, 76.3 us)
Async XLA Ops:
  7.2 180.0 %all-reduce.6.cloned.1.call-start = ((), (), s32[]{:S(2)}) async-start(), calls=%async_computation.2 | async-start | bytes 1048576 | tf_op jit(solution)/shard_map/psum | solution.py:37
  17.2 292.4 %all-reduce.10.cloned.1.call-start = ((), (), s32[]{:S(2)}) async-start(), calls=%async_computation.5 | async-start | bytes 3145728 | tf_op jit(solution)/shard_map/psum | solution.py:37
  180.8 6.4 copy-start.1
  202.9 408.5 %all-reduce.8.cloned.1.call-start = ((), (), s32[]{:S(2)}) async-start(), calls=%async_computation.4 | async-start | bytes 3145728 | tf_op jit(solution)/shard_map/psum | solution.py:37
  502.8 5.0 copy-start.3
  503.8 325.2 %all-gather.5.cloned.1.call-start = ((), (), s32[]{:S(2)}) async-start(), calls=%async_computation.3 | async-start | bytes 34603008 | tf_op jit(solution)/shard_map/all_gather | solution.py:56
  781.4 5.3 copy-start
  781.5 5.3 copy-start.2
Sparse Core Ops, SparseCore 0:
  17.3 107.8 all-reduce.5
  203.0 106.5 all-reduce.9
  503.9 107.4 all-reduce.7
  613.4 125.5 all-gather.4
